TPU v7x, 32 devices: a whole 2x2x4 slice. The times are simulated.
32 devices in a mesh: ctx: 8 (over z, x), fsdp: 4 (over y, core).
Axes of the slice: x: 2, y: 2, z: 4, core: 2. Of those that a mesh axis runs over, the one named last changes fastest.
Arguments:
- inputs: bfloat16 [2, 4, 4096, 512], P(None, 'fsdp', 'ctx'), may hold values from -6 to 6
- out_grad: bfloat16 [2, 4, 4096, 512], P(None, 'fsdp', 'ctx'), may hold values from -6 to 6
- segment_ids: int32 [2, 4, 4096], P(None, 'fsdp', 'ctx'), may hold values from 0 to 15, never falling along the last dimension, each value on 1 to 2048 neighbouring positions
- block_order: int32 [16], replicated, may hold values from 0 to 15, each once
- w_qkv: bfloat16 [512, 1536], P('fsdp'), may hold values from -0.25 to 0.25
- w_out: bfloat16 [512, 512], P('fsdp'), may hold values from -1 to 1
- w_up: bfloat16 [512, 2048], P('fsdp'), may hold values from -0.25 to 0.25
- w_down: bfloat16 [2048, 512], P('fsdp'), may hold values from -0.125 to 0.125
- norm1_gain: bfloat16 [512], P('fsdp'), may hold values from 0.25 to 1.75
- norm1_bias: bfloat16 [512], P('fsdp'), may hold values from -2 to 2
- norm2_gain: bfloat16 [512], P('fsdp'), may hold values from 0.25 to 1.75
- norm2_bias: bfloat16 [512], P('fsdp'), may hold values from -2 to 2
- out_bias: bfloat16 [512], P('fsdp'), may hold values from -2 to 2
- up_bias: bfloat16 [2048], P('fsdp'), may hold values from -3 to 3
- down_bias: bfloat16 [512], P('fsdp'), may hold values from -2 to 2
Outputs:
- outputs: bfloat16 [2, 4, 4096, 512], P(None, 'fsdp', 'ctx')
- input_grad: float32 [2, 4, 4096, 512], P(None, 'fsdp', 'ctx')
- grad_w_qkv: float32 [512, 1536], P('fsdp')
- grad_w_out: float32 [512, 512], P('fsdp')
- grad_w_up: float32 [512, 2048], P('fsdp')
- grad_w_down: float32 [2048, 512], P('fsdp')
- grad_norm1_gain: float32 [512], P('fsdp')
- grad_norm1_bias: float32 [512], P('fsdp')
- grad_norm2_gain: float32 [512], P('fsdp')
- grad_norm2_bias: float32 [512], P('fsdp')
- grad_out_bias: float32 [512], P('fsdp')
- grad_up_bias: float32 [2048], P('fsdp')
- grad_down_bias: float32 [512], P('fsdp')
Inputs may be any that keep to these rules, and one draw needn't show every extreme that they name: `segment_ids`: along each sequence's true positions document numbers start at 0 and never fall; each document has 1 to 2048 tokens and one has exactly 2048. `block_order`: each value appears exactly once.
All inputs are finite; a program needn't handle non-finite values.
Results may differ from a plain program's by a relative error of at most 0.02.
Values may be sent and summed in bfloat16 or wider, within the bound.
A program may use at most 256 MiB of HBM per device.

v0:
```python
import math
import jax
import jax.numpy as jnp
from jax import lax
from jax.sharding import PartitionSpec as P

H = 8
HD = 64
BLK = 256
norm_eps = 1e-05
mask_fill = -1e30


def layer_norm(values, gain_vec, offset):
    center = values - jnp.mean(values, axis=-1, keepdims=True)
    spread = jnp.mean(center * center, axis=-1, keepdims=True)
    return center * lax.rsqrt(spread + norm_eps) * gain_vec + offset


def gelu_exact(values):
    return 0.5 * values * (1.0 + lax.erf(values * (1.0 / math.sqrt(2.0))))


def score_block(query_heads, key_heads, query_doc, query_pos, key_doc, key_pos):
    raw_scores = jnp.einsum(
        "qhd,khd->hqk", query_heads, key_heads, preferred_element_type=jnp.float32
    ) * (1.0 / math.sqrt(HD))
    allowed = (query_doc[:, None] == key_doc[None, :]) & (key_pos[None, :] <= query_pos[:, None])
    return (raw_scores, allowed[None])


def soft_block(raw_scores, allowed, log_norm):
    return jnp.exp(jnp.where(allowed, raw_scores, mask_fill) - log_norm[:, :, None])


def row_log_norm(query_heads, key_blocks, doc_blocks, pos_blocks, query_doc, query_pos):

    def row_visit(running, block_item):
        row_top, row_sum = running
        key_heads, key_doc, key_pos = block_item
        raw_scores, allowed = score_block(
            query_heads, key_heads, query_doc, query_pos, key_doc, key_pos
        )
        masked = jnp.where(allowed, raw_scores, mask_fill)
        new_top = jnp.maximum(row_top, jnp.max(masked, axis=-1))
        fresh = jnp.sum(jnp.where(allowed, jnp.exp(masked - new_top[:, :, None]), 0.0), axis=-1)
        return ((new_top, row_sum * jnp.exp(row_top - new_top) + fresh), None)

    query_count = query_doc.shape[0]
    start = (
        jnp.full((H, query_count), mask_fill, jnp.float32),
        jnp.zeros((H, query_count), jnp.float32),
    )
    (row_top, row_sum), unused = lax.scan(row_visit, start, (key_blocks, doc_blocks, pos_blocks))
    return row_top + jnp.log(row_sum)


def attend(
    query_heads, key_blocks, value_blocks, doc_blocks, pos_blocks, query_doc, query_pos, log_norm
):

    def attend_visit(accum_out, block_item):
        key_heads, value_heads, key_doc, key_pos = block_item
        raw_scores, allowed = score_block(
            query_heads, key_heads, query_doc, query_pos, key_doc, key_pos
        )
        soft_low = soft_block(raw_scores, allowed, log_norm).astype(jnp.bfloat16)
        return (
            accum_out
            + jnp.einsum("hqk,khd->qhd", soft_low, value_heads, preferred_element_type=jnp.float32),
            None,
        )

    start = jnp.zeros(query_heads.shape, jnp.float32)
    accum_out, unused = lax.scan(
        attend_visit, start, (key_blocks, value_blocks, doc_blocks, pos_blocks)
    )
    return accum_out


def grad_block(
    query_heads,
    grad_heads,
    log_norm,
    row_delta,
    query_doc,
    query_pos,
    key_heads,
    value_heads,
    key_doc,
    key_pos,
):
    raw_scores, allowed = score_block(
        query_heads, key_heads, query_doc, query_pos, key_doc, key_pos
    )
    soft = soft_block(raw_scores, allowed, log_norm)
    grad_soft = jnp.einsum(
        "qhd,khd->hqk", grad_heads, value_heads, preferred_element_type=jnp.float32
    )
    grad_scores = (soft * (grad_soft - row_delta[:, :, None])).astype(jnp.bfloat16)
    score_scale = 1.0 / math.sqrt(HD)
    part_q = (
        jnp.einsum("hqk,khd->qhd", grad_scores, key_heads, preferred_element_type=jnp.float32)
        * score_scale
    )
    part_k = (
        jnp.einsum("hqk,qhd->khd", grad_scores, query_heads, preferred_element_type=jnp.float32)
        * score_scale
    )
    part_v = jnp.einsum(
        "hqk,qhd->khd", soft.astype(jnp.bfloat16), grad_heads, preferred_element_type=jnp.float32
    )
    return (part_q, part_k, part_v)


def body(
    inputs,
    out_grad,
    segment_ids,
    block_order,
    w_qkv,
    w_out,
    w_up,
    w_down,
    norm1_gain,
    norm1_bias,
    norm2_gain,
    norm2_bias,
    out_bias,
    up_bias,
    down_bias,
):
    gathered = (
        lax.all_gather(w_qkv, "fsdp", axis=0, tiled=True),
        lax.all_gather(w_out, "fsdp", axis=0, tiled=True),
        lax.all_gather(w_up, "fsdp", axis=0, tiled=True),
        lax.all_gather(w_down, "fsdp", axis=0, tiled=True),
        lax.all_gather(norm1_gain, "fsdp", axis=0, tiled=True),
        lax.all_gather(norm1_bias, "fsdp", axis=0, tiled=True),
        lax.all_gather(norm2_gain, "fsdp", axis=0, tiled=True),
        lax.all_gather(norm2_bias, "fsdp", axis=0, tiled=True),
        lax.all_gather(out_bias, "fsdp", axis=0, tiled=True),
        lax.all_gather(up_bias, "fsdp", axis=0, tiled=True),
        lax.all_gather(down_bias, "fsdp", axis=0, tiled=True),
    )
    full_qkv, full_out, full_up, full_down = (gathered[0], gathered[1], gathered[2], gathered[3])
    gain_one, bias_one, gain_two, bias_two, full_obias, full_ubias, full_dbias = [
        member.astype(jnp.float32) for member in gathered[4:]
    ]
    model_width = full_qkv.shape[0]
    local_rows = inputs.shape[2]
    ctx_count = lax.axis_size("ctx")
    seq_len = local_rows * ctx_count
    key_block = min(512, seq_len)
    block_count = seq_len // key_block
    ctx_index = lax.axis_index("ctx")
    row_ids = jnp.arange(local_rows, dtype=jnp.int32)
    own_blocks = lax.dynamic_slice_in_dim(block_order, 2 * ctx_index, 2)
    own_pos = own_blocks[row_ids // BLK] * BLK + row_ids % BLK
    all_ids = jnp.arange(seq_len, dtype=jnp.int32)
    all_pos = block_order[all_ids // BLK] * BLK + all_ids % BLK
    pos_blocks = all_pos.reshape(block_count, key_block)
    grad_sums = [jnp.zeros(member.shape, jnp.float32) for member in gathered]
    outputs_list = []
    input_grads = []
    for micro_idx in range(inputs.shape[0]):
        seq_in = inputs[micro_idx, 0].astype(jnp.float32)
        normed, norm1_pull = jax.vjp(layer_norm, seq_in, gain_one, bias_one)
        normed_low = normed.astype(jnp.bfloat16)
        qkv_out = jnp.dot(normed_low, full_qkv, preferred_element_type=jnp.float32).astype(
            jnp.bfloat16
        )
        query_heads = qkv_out[:, :model_width].reshape(local_rows, H, HD)
        kv_all, doc_all = (
            lax.all_gather(qkv_out[:, model_width:], "ctx", axis=0, tiled=True),
            lax.all_gather(segment_ids[micro_idx, 0], "ctx", axis=0, tiled=True),
        )
        doc_rows = doc_all[all_pos]
        query_doc = doc_all[own_pos]
        kv_heads = kv_all.reshape(block_count, key_block, 2, H, HD)
        key_blocks = kv_heads[:, :, 0]
        value_blocks = kv_heads[:, :, 1]
        doc_blocks = doc_rows.reshape(block_count, key_block)
        log_norm = row_log_norm(query_heads, key_blocks, doc_blocks, pos_blocks, query_doc, own_pos)
        attn_acc = attend(
            query_heads,
            key_blocks,
            value_blocks,
            doc_blocks,
            pos_blocks,
            query_doc,
            own_pos,
            log_norm,
        )
        attn_low = attn_acc.reshape(local_rows, model_width).astype(jnp.bfloat16)
        branch = jnp.dot(attn_low, full_out, preferred_element_type=jnp.float32) + full_obias
        middle = seq_in + branch
        normed_two, norm2_pull = jax.vjp(layer_norm, middle, gain_two, bias_two)
        normed_two_low = normed_two.astype(jnp.bfloat16)
        hidden = jnp.dot(normed_two_low, full_up, preferred_element_type=jnp.float32) + full_ubias
        active, gelu_pull = jax.vjp(gelu_exact, hidden)
        active_low = active.astype(jnp.bfloat16)
        result = middle + (
            jnp.dot(active_low, full_down, preferred_element_type=jnp.float32) + full_dbias
        )
        outputs_list.append(result.astype(jnp.bfloat16))
        grad_y = out_grad[micro_idx, 0]
        grad_y32 = grad_y.astype(jnp.float32)
        grad_sums[3] = grad_sums[3] + jnp.einsum(
            "rf,rd->fd", active_low, grad_y, preferred_element_type=jnp.float32
        )
        grad_sums[10] = grad_sums[10] + jnp.sum(grad_y32, axis=0)
        grad_active = jnp.einsum("rd,fd->rf", grad_y, full_down, preferred_element_type=jnp.float32)
        (grad_hidden,) = gelu_pull(grad_active)
        grad_hidden_low = grad_hidden.astype(jnp.bfloat16)
        grad_sums[2] = grad_sums[2] + jnp.einsum(
            "rd,rf->df", normed_two_low, grad_hidden_low, preferred_element_type=jnp.float32
        )
        grad_sums[9] = grad_sums[9] + jnp.sum(grad_hidden_low.astype(jnp.float32), axis=0)
        grad_normed_two = jnp.einsum(
            "rf,df->rd", grad_hidden_low, full_up, preferred_element_type=jnp.float32
        )
        grad_mid_ln, grad_gain_two, grad_bias_two = norm2_pull(grad_normed_two)
        grad_sums[6] = grad_sums[6] + grad_gain_two
        grad_sums[7] = grad_sums[7] + grad_bias_two
        grad_mid = grad_y32 + grad_mid_ln
        grad_mid_low = grad_mid.astype(jnp.bfloat16)
        grad_sums[1] = grad_sums[1] + jnp.einsum(
            "rd,re->de", attn_low, grad_mid_low, preferred_element_type=jnp.float32
        )
        grad_sums[8] = grad_sums[8] + jnp.sum(grad_mid_low.astype(jnp.float32), axis=0)
        grad_attn_low = jnp.einsum(
            "re,de->rd", grad_mid_low, full_out, preferred_element_type=jnp.float32
        ).astype(jnp.bfloat16)
        grad_heads = grad_attn_low.reshape(local_rows, H, HD)
        row_delta = jnp.sum(grad_heads.astype(jnp.float32) * attn_acc, axis=-1).T

        def back_visit(grad_query, block_item):
            key_heads, value_heads, key_doc, key_pos = block_item
            part_q, part_k, part_v = grad_block(
                query_heads,
                grad_heads,
                log_norm,
                row_delta,
                query_doc,
                own_pos,
                key_heads,
                value_heads,
                key_doc,
                key_pos,
            )
            joined = jnp.concatenate(
                [part_k.reshape(key_block, model_width), part_v.reshape(key_block, model_width)],
                axis=1,
            )
            return (grad_query + part_q, joined)

        grad_query, kv_terms = lax.scan(
            back_visit,
            jnp.zeros((local_rows, H, HD), jnp.float32),
            (key_blocks, value_blocks, doc_blocks, pos_blocks),
        )
        kv_grad = lax.psum_scatter(
            kv_terms.reshape(seq_len, 2 * model_width).astype(jnp.bfloat16),
            "ctx",
            scatter_dimension=0,
            tiled=True,
        ).astype(jnp.float32)
        grad_qkv_low = jnp.concatenate(
            [grad_query.reshape(local_rows, model_width), kv_grad], axis=1
        ).astype(jnp.bfloat16)
        grad_sums[0] = grad_sums[0] + jnp.einsum(
            "rd,re->de", normed_low, grad_qkv_low, preferred_element_type=jnp.float32
        )
        grad_normed = jnp.einsum(
            "re,de->rd", grad_qkv_low, full_qkv, preferred_element_type=jnp.float32
        )
        grad_in_ln, grad_gain_one, grad_bias_one = norm1_pull(grad_normed)
        grad_sums[4] = grad_sums[4] + grad_gain_one
        grad_sums[5] = grad_sums[5] + grad_bias_one
        input_grads.append(grad_mid + grad_in_ln)
    owned = (
        lax.psum_scatter(
            grad_sums[0].astype(jnp.bfloat16), "fsdp", scatter_dimension=0, tiled=True
        ).astype(jnp.float32),
        lax.psum_scatter(
            grad_sums[1].astype(jnp.bfloat16), "fsdp", scatter_dimension=0, tiled=True
        ).astype(jnp.float32),
        lax.psum_scatter(
            grad_sums[2].astype(jnp.bfloat16), "fsdp", scatter_dimension=0, tiled=True
        ).astype(jnp.float32),
        lax.psum_scatter(
            grad_sums[3].astype(jnp.bfloat16), "fsdp", scatter_dimension=0, tiled=True
        ).astype(jnp.float32),
        lax.psum_scatter(
            grad_sums[4].astype(jnp.bfloat16), "fsdp", scatter_dimension=0, tiled=True
        ).astype(jnp.float32),
        lax.psum_scatter(
            grad_sums[5].astype(jnp.bfloat16), "fsdp", scatter_dimension=0, tiled=True
        ).astype(jnp.float32),
        lax.psum_scatter(
            grad_sums[6].astype(jnp.bfloat16), "fsdp", scatter_dimension=0, tiled=True
        ).astype(jnp.float32),
        lax.psum_scatter(
            grad_sums[7].astype(jnp.bfloat16), "fsdp", scatter_dimension=0, tiled=True
        ).astype(jnp.float32),
        lax.psum_scatter(
            grad_sums[8].astype(jnp.bfloat16), "fsdp", scatter_dimension=0, tiled=True
        ).astype(jnp.float32),
        lax.psum_scatter(
            grad_sums[9].astype(jnp.bfloat16), "fsdp", scatter_dimension=0, tiled=True
        ).astype(jnp.float32),
        lax.psum_scatter(
            grad_sums[10].astype(jnp.bfloat16), "fsdp", scatter_dimension=0, tiled=True
        ).astype(jnp.float32),
    )
    summed = (
        lax.psum(owned[0].astype(jnp.bfloat16), "ctx").astype(jnp.float32),
        lax.psum(owned[1].astype(jnp.bfloat16), "ctx").astype(jnp.float32),
        lax.psum(owned[2].astype(jnp.bfloat16), "ctx").astype(jnp.float32),
        lax.psum(owned[3].astype(jnp.bfloat16), "ctx").astype(jnp.float32),
        lax.psum(owned[4].astype(jnp.bfloat16), "ctx").astype(jnp.float32),
        lax.psum(owned[5].astype(jnp.bfloat16), "ctx").astype(jnp.float32),
        lax.psum(owned[6].astype(jnp.bfloat16), "ctx").astype(jnp.float32),
        lax.psum(owned[7].astype(jnp.bfloat16), "ctx").astype(jnp.float32),
        lax.psum(owned[8].astype(jnp.bfloat16), "ctx").astype(jnp.float32),
        lax.psum(owned[9].astype(jnp.bfloat16), "ctx").astype(jnp.float32),
        lax.psum(owned[10].astype(jnp.bfloat16), "ctx").astype(jnp.float32),
    )
    return (
        jnp.stack(outputs_list)[:, None],
        jnp.stack(input_grads)[:, None],
        summed[0],
        summed[1],
        summed[2],
        summed[3],
        summed[4],
        summed[5],
        summed[6],
        summed[7],
        summed[8],
        summed[9],
        summed[10],
    )


def solution(mesh):
    return jax.shard_map(
        body,
        mesh=mesh,
        in_specs=(
            P(None, "fsdp", "ctx", None),
            P(None, "fsdp", "ctx", None),
            P(None, "fsdp", "ctx"),
            P(),
            P("fsdp", None),
            P("fsdp", None),
            P("fsdp", None),
            P("fsdp", None),
            P("fsdp"),
            P("fsdp"),
            P("fsdp"),
            P("fsdp"),
            P("fsdp"),
            P("fsdp"),
            P("fsdp"),
        ),
        out_specs=(
            P(None, "fsdp", "ctx", None),
            P(None, "fsdp", "ctx", None),
            P("fsdp", None),
            P("fsdp", None),
            P("fsdp", None),
            P("fsdp", None),
            P("fsdp"),
            P("fsdp"),
            P("fsdp"),
            P("fsdp"),
            P("fsdp"),
            P("fsdp"),
            P("fsdp"),
        ),
        check_vma=False,
    )
```

profile of v0, /device:TPU:0, one launch (start us, length us, event | category | flops | bytes accessed | tf_op | source)
XLA Modules:
  0.0 1195.3 jit_solution(4293471570105327463)
XLA Ops:
  8.0 6.2 all-gather.2
  14.1 5.4 all-gather.3
  21.4 10.5 all-gather.15.cloned.1.call-done
  45.4 27.0 %all-gather = s32[1,1,4096]{2,1,0:T(1,128)S(1)} all-gather(s32[1,1,512]{2,1,0:T(1,128)S(1)} %get-tuple-element.1148), channel_id=2, replica_groups=mesh['ctx'=8,'fsdp'=4] {'ctx'}, dimensions={2}, use_global_device_ids=true | all-gather | bytes 18432 | tf_op jit(solution)/shard_map/all_gather | solution.py:176
  76.7 5.7 select_multiply_fusion.2
  85.7 23.0 %gather_fusion.1 = s32[4096]{0:T(1024)S(1)} fusion(s32[4096]{0:T(1024)S(1)} %bitcast.527, s32[4096]{0:T(1024)S(1)} %broadcast_clamp_fusion), kind=kCustom, calls=%fused_computation.1 | custom fusion | bytes 49152 | tf_op jit(solution)/shard_map/gather | solution.py:178
  108.7 26.7 %all-gather.1 = s32[1,1,4096]{2,1,0:T(1,128)S(1)} all-gather(s32[1,1,512]{2,1,0:T(1,128)S(1)} %get-tuple-element.1149), channel_id=3, replica_groups=mesh['ctx'=8,'fsdp'=4] {'ctx'}, dimensions={2}, use_global_device_ids=true | all-gather | bytes 18432 | tf_op jit(solution)/shard_map/all_gather | solution.py:176
  138.6 23.0 %gather_fusion.3 = s32[4096]{0:T(1024)S(1)} fusion(s32[4096]{0:T(1024)S(1)} %bitcast.529, s32[4096]{0:T(1024)S(1)} %broadcast_clamp_fusion), kind=kCustom, calls=%fused_computation.3 | custom fusion | bytes 49152 | tf_op jit(solution)/shard_map/gather | solution.py:178
  182.3 7.2 all_gather.50
  195.1 11.4 copy.162
  206.6 12.2 %copy.239 = bf16[128,8,8,512]{3,2,1,0:T(8,128)(2,1)} copy(bf16[128,8,8,512]{3,1,2,0:T(8,128)(2,1)} %bitcast.538) | data formatting | bytes 16777216
  218.8 5.3 slice_bitcast_fusion
  227.5 50.1 %while.76 = (s32[]{:T(128)}, f32[8,512]{1,0:T(8,128)S(1)}, f32[8,512]{1,0:T(8,128)S(1)}, s32[512]{0:T(512)S(1)}, s32[8,512]{1,0:T(8,128)S(1)}, /*index=5*/s32[8,...) while((s32[]{:T(128)}, f32[8,512]{1,0:T(8,128)S(1)}, ...), condition=%wide.region_15.16_spmd.clone, body=%wide.region_12.15_spmd.clone.sunk | while | flops 286030336 | bytes 18847896 | solution.py:54
  277.6 10.2 all-gather.17.cloned.1.call-done
  287.8 11.7 copy.155
  299.6 12.2 %copy.238 = bf16[128,8,8,512]{3,2,1,0:T(8,128)(2,1)} copy(bf16[128,8,8,512]{3,1,2,0:T(8,128)(2,1)} %bitcast.539) | data formatting | bytes 16777216
  320.5 50.5 %while.74 = (s32[]{:T(128)}, f32[8,512]{1,0:T(8,128)S(1)}, f32[8,512]{1,0:T(8,128)S(1)}, s32[512]{0:T(512)S(1)}, s32[8,512]{1,0:T(8,128)S(1)}, /*index=5*/s32[8,...) while((s32[]{:T(128)}, f32[8,512]{1,0:T(8,128)S(1)}, ...), condition=%wide.region_5.6_spmd.clone, body=%wide.region_2.5_spmd.clone.sunk | while | flops 286030336 | bytes 18847896 | solution.py:54
  371.0 5.7 copy.158
  377.3 46.4 %while.75 = (s32[]{:T(128)}, f32[512,8,64]{0,2,1:T(8,128)S(1)}, bf16[8,512,8,64]{1,3,2,0:T(8,128)(2,1)}, s32[512]{0:T(512)S(1)}, s32[8,512]{1,0:T(8,128)S(1)}, /...) while((s32[]{:T(128)}, f32[512,8,64]{0,2,1:T(8,128)S(1)}, ...), condition=%wide.region_7.8_spmd.clone, body=%wide.region_6.7_spmd.clone.sunk | while | flops 546580992 | bytes 4234906 | solution.py:75
  424.7 5.7 copy.165
  430.4 46.4 %while.77 = (s32[]{:T(128)}, f32[512,8,64]{0,2,1:T(8,128)S(1)}, bf16[8,512,8,64]{1,3,2,0:T(8,128)(2,1)}, s32[512]{0:T(512)S(1)}, s32[8,512]{1,0:T(8,128)S(1)}, /...) while((s32[]{:T(128)}, f32[512,8,64]{0,2,1:T(8,128)S(1)}, ...), condition=%wide.region_17.18_spmd.clone, body=%wide.region_16.17_spmd.clone.sunk | while | flops 546580992 | bytes 4234906 | solution.py:75
  486.4 5.9 convert_reduce_fusion
  497.7 6.1 multiply_convert_fusion.1
  525.5 138.9 %while.78 = (s32[]{:T(128)}, f32[512,8,64]{0,2,1:T(8,128)}, bf16[8,512,1024]{2,1,0:T(8,128)(2,1)}, bf16[8,512,8,64]{1,3,2,0:T(8,128)(2,1)}, s32[512]{0:T(512)S(1...) while((s32[]{:T(128)}, f32[512,8,64]{0,2,1:T(8,128)}, ...), condition=%wide.region_24.25_spmd.clone, body=%wide.region_23.24_spmd.clone.sunk | while | flops 1367353856 | bytes 51714240 | solution.py:258
  668.7 131.5 %while.79 = (s32[]{:T(128)}, f32[512,8,64]{0,2,1:T(8,128)}, bf16[8,512,1024]{2,1,0:T(8,128)(2,1)}, bf16[8,512,8,64]{1,3,2,0:T(8,128)(2,1)}, s32[512]{0:T(512)S(1...) while((s32[]{:T(128)}, f32[512,8,64]{0,2,1:T(8,128)}, ...), condition=%wide.region_32.33_spmd.clone, body=%wide.region_31.32_spmd.clone.sunk | while | flops 1367353856 | bytes 51714240 | solution.py:258
  834.8 129.0 %reduce-scatter.9.cloned.1.call-done = bf16[512,1024]{1,0:T(8,128)(2,1)} async-done(((bf16[4096,1024]{1,0:T(8,128)(2,1)}), bf16[512,1024]{1,0:T(8,128)(2,1)}) %reduce-scatter.9.cloned.1.call-update) | async-done | bytes 1048592 | tf_op jit(solution)/shard_map/reduce_scatter | solution.py:263
  987.0 34.2 %reduce-scatter.15.cloned.1.call-done = bf16[128,2048]{1,0:T(8,128)(2,1)} async-done(((bf16[512,2048]{1,0:T(8,128)(2,1)}), bf16[128,2048]{1,0:T(8,128)(2,1)}) %reduce-scatter.15.cloned.1.call-update) | async-done | bytes 524304 | tf_op jit(solution)/shard_map/reduce_scatter | solution.py:289
  1021.1 33.9 %reduce-scatter.17.cloned.1.call-done = bf16[512,512]{1,0:T(8,128)(2,1)} async-done(((bf16[2048,512]{1,0:T(8,128)(2,1)}), bf16[512,512]{1,0:T(8,128)(2,1)}) %reduce-scatter.17.cloned.1.call-update) | async-done | bytes 524304 | tf_op jit(solution)/shard_map/reduce_scatter | solution.py:292
  1055.0 31.5 %reduce-scatter.11.cloned.1.call-done = bf16[128,1536]{1,0:T(8,128)(2,1)} async-done(((bf16[512,1536]{1,0:T(8,128)(2,1)}), bf16[128,1536]{1,0:T(8,128)(2,1)}) %reduce-scatter.11.cloned.1.call-update) | async-done | bytes 393232 | tf_op jit(solution)/shard_map/reduce_scatter | solution.py:283
  1091.7 10.5 all-reduce.9
  1102.8 22.1 %all-reduce.7 = (bf16[128]{0:T(256)(128)(2,1)S(1)}, bf16[128]{0:T(256)(128)(2,1)S(1)}, bf16[128]{0:T(256)(128)(2,1)S(1)}, bf16[128]{0:T(256)(128)(2,1)S(1)}, bf1...) all-reduce(bf16[128]{0:T(256)(128)(2,1)S(1)} %dynamic-slice.1, ...), channel_id=1, replica_groups=mesh['ctx'=8,'fsdp'=4] {'ctx'}, use_global_device_ids=true, to_apply=%region_47.48 | all-reduce | flops 1280 | bytes 5120 | tf_op jit(solution)/shard_map/psum | solution.py:322
  1131.7 48.7 %all-reduce.12.cloned.1.call-done = (bf16[128,1536]{1,0:T(8,128)(2,1)}, bf16[128,512]{1,0:T(8,128)(2,1)}, bf16[128,2048]{1,0:T(8,128)(2,1)}, bf16[512,512]{1,0:T(8,128)(2,1)}) async-done(((bf16[128,1536]{1,0:T(8,128)(2,1)}, bf16[128,512]{1,0:T(8,128)(2,1)}, bf16[128,2048]{1,0:T(8,128)(2,1)}, bf16[512,512]{1,0:T(8,128)(2,1)}), (bf16[128,1536]{1,0:T(8,128)(2,1)}, bf16[128,512]{1,0:T(8,128)(2,1)}, ...) | async-done | bytes 1572880 | tf_op jit(solution)/shard_map/psum | solution.py:318
  (799 shorter events, 643.1 us)
Async XLA Ops:
  7.2 24.8 %all-gather.15.cloned.1.call-start = ((), (), s32[]{:S(2)}) async-start(), calls=%async_computation.6 | async-start | bytes 1966080 | tf_op jit(solution)/shard_map/all_gather | solution.py:134
  7.9 187.2 %all-gather.23.cloned.1.call-start = ((), (), s32[]{:S(2)}) async-start(), calls=%async_computation.10 | async-start | bytes 9437184 | tf_op jit(solution)/shard_map/all_gather | solution.py:175
  36.8 251.0 %all-gather.17.cloned.1.call-start = ((), (), s32[]{:S(2)}) async-start(), calls=%async_computation.7 | async-start | bytes 9437184 | tf_op jit(solution)/shard_map/all_gather | solution.py:175
  37.1 441.5 %copy-start.7 = (bf16[1,1,512,512]{2,3,1,0:T(8,128)(2,1)}, bf16[1,1,512,512]{2,3,1,0:T(8,128)(2,1)S(1)}, u32[]{:S(2)}) copy-start(bf16[1,1,512,512]{2,3,1,0:T(8,128)(2,1)S(1)} %copy.202) | copy-start | bytes 1572868
  40.9 440.4 %all-gather.19.cloned.1.call-start = ((), (), s32[]{:S(2)}) async-start(), calls=%async_computation.8 | async-start | bytes 2621440 | tf_op jit(solution)/shard_map/all_gather | solution.py:136
  41.5 444.9 %all-gather.21.cloned.1.call-start = ((), (), s32[]{:S(2)}) async-start(), calls=%async_computation.9 | async-start | bytes 2621440 | tf_op jit(solution)/shard_map/all_gather | solution.py:137
  42.1 788.4 %reduce-scatter.7.cloned.1.call-start = ((), (), s32[]{:S(2)}) async-start(), calls=%async_computation.11 | async-start | bytes 9437184 | tf_op jit(solution)/shard_map/reduce_scatter | solution.py:263
  138.6 38.4 %copy-start.91 = (bf16[512]{0:T(512)(128)(2,1)S(1)}, bf16[512]{0:T(512)(128)(2,1)}, u32[]{:S(2)}) copy-start(bf16[512]{0:T(512)(128)(2,1)} %param.40) | copy-start | bytes 3076
  138.6 43.7 %copy-start.51 = (bf16[128,512]{1,0:T(8,128)(2,1)S(1)}, bf16[128,512]{1,0:T(8,128)(2,1)}, u32[]{:S(2)}) copy-start(bf16[128,512]{1,0:T(8,128)(2,1)} %param.32) | copy-start | bytes 393220
  138.6 50.9 %copy-start.28 = (bf16[2,1,512,512]{3,2,1,0:T(8,128)(2,1)S(1)}, bf16[2,1,512,512]{3,2,1,0:T(8,128)(2,1)}, u32[]{:S(2)}) copy-start(bf16[2,1,512,512]{3,2,1,0:T(8,128)(2,1)} %param.28) | copy-start | bytes 3145732
  167.0 349.0 %copy-start.47 = (f32[4,1,128]{2,1,0:T(1,128)}, f32[4,1,128]{2,1,0:T(1,128)S(1)}, u32[]{:S(2)}) copy-start(f32[4,1,128]{2,1,0:T(1,128)S(1)} %convert_element_type.307) | copy-start | bytes 6148
  172.0 325.7 %copy-start.53 = (f32[4,1,128]{2,1,0:T(1,128)}, f32[4,1,128]{2,1,0:T(1,128)S(1)}, u32[]{:S(2)}) copy-start(f32[4,1,128]{2,1,0:T(1,128)S(1)} %convert_element_type.308) | copy-start | bytes 6148
  189.5 289.0 %copy-start.9 = (bf16[512,512]{1,0:T(8,128)(2,1)}, bf16[512,512]{1,0:T(8,128)(2,1)S(1)}, u32[]{:S(2)}) copy-start(bf16[512,512]{1,0:T(8,128)(2,1)S(1)} %all_gather.50) | copy-start | bytes 1572868
  479.1 36.9 %copy-start.2 = (f32[512,512]{0,1:T(8,128)}, f32[512,512]{0,1:T(8,128)S(1)}, u32[]{:S(2)}) copy-start(f32[512,512]{0,1:T(8,128)S(1)} %get-tuple-element.1175) | copy-start | bytes 3145732
  479.1 36.9 %copy-start.57 = (f32[512]{0:T(512)}, f32[512]{0:T(512)S(1)}, u32[]{:S(2)}) copy-start(f32[512]{0:T(512)S(1)} %broadcast_multiply_fusion.2) | copy-start | bytes 6148
  481.0 35.0 %copy-start = (f32[512,512]{0,1:T(8,128)}, f32[512,512]{0,1:T(8,128)S(1)}, u32[]{:S(2)}) copy-start(f32[512,512]{0,1:T(8,128)S(1)} %get-tuple-element.1177) | copy-start | bytes 3145732
  481.1 35.0 %copy-start.49 = (f32[512]{0:T(512)}, f32[512]{0:T(512)S(1)}, u32[]{:S(2)}) copy-start(f32[512]{0:T(512)S(1)} %broadcast_multiply_fusion) | copy-start | bytes 6148
  481.3 34.8 %copy-start.55 = (f32[512]{0:T(512)}, f32[512]{0:T(512)S(1)}, u32[]{:S(2)}) copy-start(f32[512]{0:T(512)S(1)} %get-tuple-element.1196) | copy-start | bytes 6148
  481.3 34.8 %copy-start.65 = (f32[512]{0:T(512)}, f32[512]{0:T(512)S(1)}, u32[]{:S(2)}) copy-start(f32[512]{0:T(512)S(1)} %get-tuple-element.1195) | copy-start | bytes 6148
  664.4 299.4 %reduce-scatter.9.cloned.1.call-start = ((), (), s32[]{:S(2)}) async-start(), calls=%async_computation.12 | async-start | bytes 9437184 | tf_op jit(solution)/shard_map/reduce_scatter | solution.py:263
  800.3 186.7 %reduce-scatter.13.cloned.1.call-start = ((), (), s32[]{:S(2)}) async-start(), calls=%async_computation.14 | async-start | bytes 655360 | tf_op jit(solution)/shard_map/reduce_scatter | solution.py:286
  803.2 218.0 %reduce-scatter.15.cloned.1.call-start = ((), (), s32[]{:S(2)}) async-start(), calls=%async_computation.15 | async-start | bytes 2621440 | tf_op jit(solution)/shard_map/reduce_scatter | solution.py:289
  809.2 245.8 %reduce-scatter.17.cloned.1.call-start = ((), (), s32[]{:S(2)}) async-start(), calls=%async_computation.16 | async-start | bytes 2621440 | tf_op jit(solution)/shard_map/reduce_scatter | solution.py:292
  815.1 271.4 %reduce-scatter.11.cloned.1.call-start = ((), (), s32[]{:S(2)}) async-start(), calls=%async_computation.13 | async-start | bytes 1966080 | tf_op jit(solution)/shard_map/reduce_scatter | solution.py:283
  830.5 133.3 %copy-start.6 = (bf16[1,1,512,512]{2,3,1,0:T(8,128)(2,1)S(1)}, bf16[1,1,512,512]{2,3,1,0:T(8,128)(2,1)}, u32[]{:S(2)}) copy-start(bf16[1,1,512,512]{2,3,1,0:T(8,128)(2,1)} %copy-done.4) | copy-start | bytes 1572868
  830.5 133.3 %copy-start.62 = (f32[512]{0:T(512)S(1)}, f32[512]{0:T(512)}, u32[]{:S(2)}) copy-start(f32[512]{0:T(512)} %copy-done.61) | copy-start | bytes 6148
  830.5 133.3 %copy-start.68 = (f32[512]{0:T(512)S(1)}, f32[512]{0:T(512)}, u32[]{:S(2)}) copy-start(f32[512]{0:T(512)} %copy-done.67) | copy-start | bytes 6148
  968.2 212.2 %all-reduce.12.cloned.1.call-start = ((), (), s32[]{:S(2)}) async-start(), calls=%async_computation.17 | async-start | bytes 3145728 | tf_op jit(solution)/shard_map/psum | solution.py:318
  981.3 105.2 %copy-start.27 = (bf16[1,1,512,512]{2,3,1,0:T(8,128)(2,1)S(1)}, bf16[1,1,512,512]{2,3,1,0:T(8,128)(2,1)}, u32[]{:S(2)}) copy-start(bf16[1,1,512,512]{2,3,1,0:T(8,128)(2,1)} %copy.204) | copy-start | bytes 1572868
  981.3 105.2 %copy-start.78 = (f32[512]{0:T(512)S(1)}, f32[512]{0:T(512)}, u32[]{:S(2)}) copy-start(f32[512]{0:T(512)} %copy-done.77) | copy-start | bytes 6148
  986.3 103.6 %copy-start.23 = (bf16[1,1,512,512]{2,3,1,0:T(8,128)(2,1)S(1)}, bf16[1,1,512,512]{2,3,1,0:T(8,128)(2,1)}, u32[]{:S(2)}) copy-start(bf16[1,1,512,512]{2,3,1,0:T(8,128)(2,1)} %copy.205) | copy-start | bytes 1572868
  986.3 103.6 %copy-start.76 = (f32[512]{0:T(512)S(1)}, f32[512]{0:T(512)}, u32[]{:S(2)}) copy-start(f32[512]{0:T(512)} %copy-done.75) | copy-start | bytes 6148
  (80 other events, 435.9 us)
Sparse Core Ops, SparseCore 0:
  9.6 22.3 all-gather.14
  36.9 125.5 all-gather.22
  164.7 123.0 all-gather.16
  289.2 20.7 all-gather.18
  311.5 22.5 all-gather.20
  664.5 147.1 reduce-scatter.6
  815.8 147.9 reduce-scatter.8
  966.3 20.6 reduce-scatter.12
  989.7 31.4 reduce-scatter.14
  1023.5 31.4 reduce-scatter.16
  1058.3 28.1 reduce-scatter.10
  1090.2 90.2 all-reduce.11
where the time goes:
time: 1210 us; the launch traced here: 1200 us
  matrix products  395 us (33%)
  waiting for transfers between devices  301 us (25%)
  local copies, waits for them, and re-layouts  193 us (16%)
  other arithmetic  155 us (13%)
  blocking collectives  131 us (11%)
  between operations  17.2 us (1%)
    reduce_scatter x2, waiting for transfers between devices, body(): lax.psum_scatter(kv_terms.reshape(seq_len, 2 * model_width).astype(jnp.bf...  129 us
    dot_general x32, matrix products, score_block(): jnp.einsum('qhd,khd->hqk', query_heads, key_heads, preferred_element_type...  77.9 us
    dot_general x16, matrix products, attend_visit(): jnp.einsum('hqk,khd->qhd', soft_low, value_heads, preferred_element_type=...  66.4 us
    dot_general x16, matrix products, grad_block(): jnp.einsum('qhd,khd->hqk', grad_heads, value_heads, preferred_element_typ...  64.5 us
    mul x48, other arithmetic, body(): own_pos = own_blocks[row_ids // BLK] * BLK + row_ids % BLK  62.6 us
    unnamed x219, local copies, waits for them, and re-layouts  55.3 us
    all_gather x2, blocking collectives, body(): lax.all_gather(segment_ids[micro_idx, 0], 'ctx', axis=0, tiled=True)  53.6 us
    dot_general x16, matrix products, grad_block(): jnp.einsum('hqk,khd->qhd', grad_scores, key_heads, preferred_element_type...  50 us
  transfers between devices with their start and end apart: 12, of which 8 were waited for; matrix products, arithmetic and copies ran while one was open for 46% of the time, Pallas kernels for 0%

commit v1 on v0

--- a/solution.py
+++ b/solution.py
@@ -315,7 +315,7 @@
         ).astype(jnp.float32),
     )
     summed = (
-        lax.psum(owned[0].astype(jnp.bfloat16), "ctx").astype(jnp.float32),
+        jnp.sum(lax.all_gather(owned[0].astype(jnp.bfloat16), "ctx"), axis=0).astype(jnp.float32),
         lax.psum(owned[1].astype(jnp.bfloat16), "ctx").astype(jnp.float32),
         lax.psum(owned[2].astype(jnp.bfloat16), "ctx").astype(jnp.float32),
         lax.psum(owned[3].astype(jnp.bfloat16), "ctx").astype(jnp.float32),

time: 1210 us -> 1260 us (1.041)
  waiting for transfers between devices: 301 us -> 354 us
    psum x1, waiting for transfers between devices: 48.7 us -> 70.8 us  [body(): lax.psum(owned[1].astype(jnp.bfloat16), 'ctx').astype(jnp.float32)]
    reduce_scatter x1, waiting for transfers between devices: 0.6 us -> 19.1 us  [body(): lax.psum_scatter(grad_sums[1].astype(jnp.bfloat16), 'fsdp', scatter_dimen...]
    unnamed x219 -> x225, local copies, waits for them, and re-layouts: 55.3 us -> 55.7 us
  transfers between devices with their start and end apart: 12 -> 13, of which waited for: 8 -> 9; matrix products, arithmetic and copies ran while one was open for 46% -> 44% of each run, Pallas kernels for 0% -> 0%
where the time goes in v1:
time: 1260 us; the launch traced here: 1240 us
  matrix products  393 us (31%)
  waiting for transfers between devices  354 us (28%)
  local copies, waits for them, and re-layouts  195 us (15%)
  other arithmetic  153 us (12%)
  blocking collectives  129 us (10%)
  between operations  16.9 us (1%)
    reduce_scatter x2, waiting for transfers between devices, body(): lax.psum_scatter(kv_terms.reshape(seq_len, 2 * model_width).astype(jnp.bf...  138 us
    dot_general x32, matrix products, score_block(): jnp.einsum('qhd,khd->hqk', query_heads, key_heads, preferred_element_type...  77.9 us
    psum x1, waiting for transfers between devices, body(): lax.psum(owned[1].astype(jnp.bfloat16), 'ctx').astype(jnp.float32)  70.8 us
    dot_general x16, matrix products, attend_visit(): jnp.einsum('hqk,khd->qhd', soft_low, value_heads, preferred_element_type=...  66.4 us
    dot_general x16, matrix products, grad_block(): jnp.einsum('qhd,khd->hqk', grad_heads, value_heads, preferred_element_typ...  64.4 us
    mul x48, other arithmetic, body(): own_pos = own_blocks[row_ids // BLK] * BLK + row_ids % BLK  62.6 us
    unnamed x225, local copies, waits for them, and re-layouts  55.7 us
    all_gather x2, blocking collectives, body(): lax.all_gather(segment_ids[micro_idx, 0], 'ctx', axis=0, tiled=True)  53.5 us
  transfers between devices with their start and end apart: 13, of which 9 were waited for; matrix products, arithmetic and copies ran while one was open for 44% of the time, Pallas kernels for 0%

profile of v1, /device:TPU:0, one launch (start us, length us, event | category | flops | bytes accessed | tf_op | source)
XLA Modules:
  0.0 1244.4 jit_solution(16536931727020067586)
XLA Ops:
  8.0 6.2 all-gather.3
  14.1 5.4 all-gather.4
  21.4 10.5 all-gather.17.cloned.1.call-done
  45.4 27.0 %all-gather = s32[1,1,4096]{2,1,0:T(1,128)S(1)} all-gather(s32[1,1,512]{2,1,0:T(1,128)S(1)} %get-tuple-element.1147), channel_id=2, replica_groups=mesh['ctx'=8,'fsdp'=4] {'ctx'}, dimensions={2}, use_global_device_ids=true | all-gather | bytes 18432 | tf_op jit(solution)/shard_map/all_gather | solution.py:176
  76.6 5.8 select_multiply_fusion.2
  85.7 23.0 %gather_fusion.1 = s32[4096]{0:T(1024)S(1)} fusion(s32[4096]{0:T(1024)S(1)} %bitcast.528, s32[4096]{0:T(1024)S(1)} %broadcast_clamp_fusion), kind=kCustom, calls=%fused_computation.1 | custom fusion | bytes 49152 | tf_op jit(solution)/shard_map/gather | solution.py:178
  108.7 26.5 %all-gather.1 = s32[1,1,4096]{2,1,0:T(1,128)S(1)} all-gather(s32[1,1,512]{2,1,0:T(1,128)S(1)} %get-tuple-element.1148), channel_id=3, replica_groups=mesh['ctx'=8,'fsdp'=4] {'ctx'}, dimensions={2}, use_global_device_ids=true | all-gather | bytes 18432 | tf_op jit(solution)/shard_map/all_gather | solution.py:176
  138.4 23.0 %gather_fusion.3 = s32[4096]{0:T(1024)S(1)} fusion(s32[4096]{0:T(1024)S(1)} %bitcast.530, s32[4096]{0:T(1024)S(1)} %broadcast_clamp_fusion), kind=kCustom, calls=%fused_computation.3 | custom fusion | bytes 49152 | tf_op jit(solution)/shard_map/gather | solution.py:178
  182.1 7.2 all_gather.56
  194.9 11.6 copy.162
  206.5 12.2 copy.239
  227.4 50.1 %while.76 = (s32[]{:T(128)}, f32[8,512]{1,0:T(8,128)S(1)}, f32[8,512]{1,0:T(8,128)S(1)}, s32[512]{0:T(512)S(1)}, s32[8,512]{1,0:T(8,128)S(1)}, /*index=5*/s32[8,...) while((s32[]{:T(128)}, f32[8,512]{1,0:T(8,128)S(1)}, ...), condition=%wide.region_15.16_spmd.clone, body=%wide.region_12.15_spmd.clone.sunk | while | flops 286030336 | bytes 18847896 | solution.py:54
  277.5 10.3 all-gather.19.cloned.1.call-done
  287.8 12.0 copy.155
  299.9 12.3 copy.238
  320.8 50.5 %while.74 = (s32[]{:T(128)}, f32[8,512]{1,0:T(8,128)S(1)}, f32[8,512]{1,0:T(8,128)S(1)}, s32[512]{0:T(512)S(1)}, s32[8,512]{1,0:T(8,128)S(1)}, /*index=5*/s32[8,...) while((s32[]{:T(128)}, f32[8,512]{1,0:T(8,128)S(1)}, ...), condition=%wide.region_5.6_spmd.clone, body=%wide.region_2.5_spmd.clone.sunk | while | flops 286030336 | bytes 18847896 | solution.py:54
  371.3 5.7 copy.158
  377.6 46.4 %while.75 = (s32[]{:T(128)}, f32[512,8,64]{0,2,1:T(8,128)S(1)}, bf16[8,512,8,64]{1,3,2,0:T(8,128)(2,1)}, s32[512]{0:T(512)S(1)}, s32[8,512]{1,0:T(8,128)S(1)}, /...) while((s32[]{:T(128)}, f32[512,8,64]{0,2,1:T(8,128)S(1)}, ...), condition=%wide.region_7.8_spmd.clone, body=%wide.region_6.7_spmd.clone.sunk | while | flops 546580992 | bytes 4234906 | solution.py:75
  425.0 5.7 copy.165
  430.7 46.4 %while.77 = (s32[]{:T(128)}, f32[512,8,64]{0,2,1:T(8,128)S(1)}, bf16[8,512,8,64]{1,3,2,0:T(8,128)(2,1)}, s32[512]{0:T(512)S(1)}, s32[8,512]{1,0:T(8,128)S(1)}, /...) while((s32[]{:T(128)}, f32[512,8,64]{0,2,1:T(8,128)S(1)}, ...), condition=%wide.region_17.18_spmd.clone, body=%wide.region_16.17_spmd.clone.sunk | while | flops 546580992 | bytes 4234906 | solution.py:75
  486.8 5.9 convert_reduce_fusion
  498.1 6.1 multiply_convert_fusion.1
  525.8 139.2 %while.78 = (s32[]{:T(128)}, f32[512,8,64]{0,2,1:T(8,128)}, bf16[8,512,1024]{2,1,0:T(8,128)(2,1)}, bf16[8,512,8,64]{1,3,2,0:T(8,128)(2,1)}, s32[512]{0:T(512)S(1...) while((s32[]{:T(128)}, f32[512,8,64]{0,2,1:T(8,128)}, ...), condition=%wide.region_24.25_spmd.clone, body=%wide.region_23.24_spmd.clone.sunk | while | flops 1367353856 | bytes 51714240 | solution.py:258
  669.4 131.5 %while.79 = (s32[]{:T(128)}, f32[512,8,64]{0,2,1:T(8,128)}, bf16[8,512,1024]{2,1,0:T(8,128)(2,1)}, bf16[8,512,8,64]{1,3,2,0:T(8,128)(2,1)}, s32[512]{0:T(512)S(1...) while((s32[]{:T(128)}, f32[512,8,64]{0,2,1:T(8,128)}, ...), condition=%wide.region_32.33_spmd.clone, body=%wide.region_31.32_spmd.clone.sunk | while | flops 1367353856 | bytes 51714240 | solution.py:258
  826.8 137.7 %reduce-scatter.9.cloned.1.call-done = bf16[512,1024]{1,0:T(8,128)(2,1)} async-done(((bf16[4096,1024]{1,0:T(8,128)(2,1)}), bf16[512,1024]{1,0:T(8,128)(2,1)}) %reduce-scatter.9.cloned.1.call-update) | async-done | bytes 1048592 | tf_op jit(solution)/shard_map/reduce_scatter | solution.py:263
  969.2 19.1 %reduce-scatter.13.cloned.1.call-done = bf16[128,512]{1,0:T(8,128)(2,1)} async-done(((bf16[512,512]{1,0:T(8,128)(2,1)}), bf16[128,512]{1,0:T(8,128)(2,1)}) %reduce-scatter.13.cloned.1.call-update) | async-done | bytes 131088 | tf_op jit(solution)/shard_map/reduce_scatter | solution.py:286
  988.2 34.2 %reduce-scatter.15.cloned.1.call-done = bf16[128,2048]{1,0:T(8,128)(2,1)} async-done(((bf16[512,2048]{1,0:T(8,128)(2,1)}), bf16[128,2048]{1,0:T(8,128)(2,1)}) %reduce-scatter.15.cloned.1.call-update) | async-done | bytes 524304 | tf_op jit(solution)/shard_map/reduce_scatter | solution.py:289
  1022.4 33.9 %reduce-scatter.17.cloned.1.call-done = bf16[512,512]{1,0:T(8,128)(2,1)} async-done(((bf16[2048,512]{1,0:T(8,128)(2,1)}), bf16[512,512]{1,0:T(8,128)(2,1)}) %reduce-scatter.17.cloned.1.call-update) | async-done | bytes 524304 | tf_op jit(solution)/shard_map/reduce_scatter | solution.py:292
  1056.3 30.8 %reduce-scatter.11.cloned.1.call-done = bf16[128,1536]{1,0:T(8,128)(2,1)} async-done(((bf16[512,1536]{1,0:T(8,128)(2,1)}), bf16[128,1536]{1,0:T(8,128)(2,1)}) %reduce-scatter.11.cloned.1.call-update) | async-done | bytes 393232 | tf_op jit(solution)/shard_map/reduce_scatter | solution.py:283
  1100.9 70.8 %all-reduce.12.cloned.1.call-done = (bf16[128,512]{1,0:T(8,128)(2,1)}, bf16[128,2048]{1,0:T(8,128)(2,1)}, bf16[512,512]{1,0:T(8,128)(2,1)}) async-done(((bf16[128,512]{1,0:T(8,128)(2,1)}, bf16[128,2048]{1,0:T(8,128)(2,1)}, bf16[512,512]{1,0:T(8,128)(2,1)}), (bf16[128,512]{1,0:T(8,128)(2,1)}, bf16[128,2048]{1,0:T(8,128)(2,1)}, bf16[512,512]{1,0:T(8,128)(2,1)})) %all-reduce.12.cloned.1.call-update) | async-done | bytes 1179664 | tf_op jit(solution)/shard_map/psum | solution.py:319
  1191.0 11.3 all-reduce.9
  1202.8 19.7 %all-reduce.7 = (bf16[128]{0:T(256)(128)(2,1)S(1)}, bf16[128]{0:T(256)(128)(2,1)S(1)}, bf16[128]{0:T(256)(128)(2,1)S(1)}, bf16[128]{0:T(256)(128)(2,1)S(1)}, bf1...) all-reduce(bf16[128]{0:T(256)(128)(2,1)S(1)} %dynamic-slice.1, ...), channel_id=1, replica_groups=mesh['ctx'=8,'fsdp'=4] {'ctx'}, use_global_device_ids=true, to_apply=%region_47.48 | all-reduce | flops 1280 | bytes 5120 | tf_op jit(solution)/shard_map/psum | solution.py:322
  (809 shorter events, 649.7 us)
Async XLA Ops:
  7.2 24.8 %all-gather.17.cloned.1.call-start = ((), (), s32[]{:S(2)}) async-start(), calls=%async_computation.6 | async-start | bytes 1966080 | tf_op jit(solution)/shard_map/all_gather | solution.py:134
  7.9 187.0 %all-gather.25.cloned.1.call-start = ((), (), s32[]{:S(2)}) async-start(), calls=%async_computation.10 | async-start | bytes 9437184 | tf_op jit(solution)/shard_map/all_gather | solution.py:175
  36.8 251.0 %all-gather.19.cloned.1.call-start = ((), (), s32[]{:S(2)}) async-start(), calls=%async_computation.7 | async-start | bytes 9437184 | tf_op jit(solution)/shard_map/all_gather | solution.py:175
  37.1 441.9 %copy-start.7 = (bf16[1,1,512,512]{2,3,1,0:T(8,128)(2,1)}, bf16[1,1,512,512]{2,3,1,0:T(8,128)(2,1)S(1)}, u32[]{:S(2)}) copy-start(bf16[1,1,512,512]{2,3,1,0:T(8,128)(2,1)S(1)} %copy.202) | copy-start | bytes 1572868
  40.9 440.8 %all-gather.21.cloned.1.call-start = ((), (), s32[]{:S(2)}) async-start(), calls=%async_computation.8 | async-start | bytes 2621440 | tf_op jit(solution)/shard_map/all_gather | solution.py:136
  41.5 445.3 %all-gather.23.cloned.1.call-start = ((), (), s32[]{:S(2)}) async-start(), calls=%async_computation.9 | async-start | bytes 2621440 | tf_op jit(solution)/shard_map/all_gather | solution.py:137
  42.0 780.5 %reduce-scatter.7.cloned.1.call-start = ((), (), s32[]{:S(2)}) async-start(), calls=%async_computation.11 | async-start | bytes 9437184 | tf_op jit(solution)/shard_map/reduce_scatter | solution.py:263
  138.4 38.4 %copy-start.93 = (bf16[512]{0:T(512)(128)(2,1)S(1)}, bf16[512]{0:T(512)(128)(2,1)}, u32[]{:S(2)}) copy-start(bf16[512]{0:T(512)(128)(2,1)} %param.40) | copy-start | bytes 3076
  138.4 43.7 %copy-start.53 = (bf16[128,512]{1,0:T(8,128)(2,1)S(1)}, bf16[128,512]{1,0:T(8,128)(2,1)}, u32[]{:S(2)}) copy-start(bf16[128,512]{1,0:T(8,128)(2,1)} %param.32) | copy-start | bytes 393220
  138.4 50.9 %copy-start.31 = (bf16[2,1,512,512]{3,2,1,0:T(8,128)(2,1)S(1)}, bf16[2,1,512,512]{3,2,1,0:T(8,128)(2,1)}, u32[]{:S(2)}) copy-start(bf16[2,1,512,512]{3,2,1,0:T(8,128)(2,1)} %param.28) | copy-start | bytes 3145732
  166.7 349.6 %copy-start.49 = (f32[4,1,128]{2,1,0:T(1,128)}, f32[4,1,128]{2,1,0:T(1,128)S(1)}, u32[]{:S(2)}) copy-start(f32[4,1,128]{2,1,0:T(1,128)S(1)} %convert_element_type.309) | copy-start | bytes 6148
  171.8 326.3 %copy-start.55 = (f32[4,1,128]{2,1,0:T(1,128)}, f32[4,1,128]{2,1,0:T(1,128)S(1)}, u32[]{:S(2)}) copy-start(f32[4,1,128]{2,1,0:T(1,128)S(1)} %convert_element_type.310) | copy-start | bytes 6148
  189.3 289.6 %copy-start.9 = (bf16[512,512]{1,0:T(8,128)(2,1)}, bf16[512,512]{1,0:T(8,128)(2,1)S(1)}, u32[]{:S(2)}) copy-start(bf16[512,512]{1,0:T(8,128)(2,1)S(1)} %all_gather.56) | copy-start | bytes 1572868
  479.5 36.9 %copy-start.2 = (f32[512,512]{0,1:T(8,128)}, f32[512,512]{0,1:T(8,128)S(1)}, u32[]{:S(2)}) copy-start(f32[512,512]{0,1:T(8,128)S(1)} %get-tuple-element.1174) | copy-start | bytes 3145732
  479.5 36.9 %copy-start.59 = (f32[512]{0:T(512)}, f32[512]{0:T(512)S(1)}, u32[]{:S(2)}) copy-start(f32[512]{0:T(512)S(1)} %broadcast_multiply_fusion.2) | copy-start | bytes 6148
  481.4 35.0 %copy-start = (f32[512,512]{0,1:T(8,128)}, f32[512,512]{0,1:T(8,128)S(1)}, u32[]{:S(2)}) copy-start(f32[512,512]{0,1:T(8,128)S(1)} %get-tuple-element.1176) | copy-start | bytes 3145732
  481.4 35.0 %copy-start.51 = (f32[512]{0:T(512)}, f32[512]{0:T(512)S(1)}, u32[]{:S(2)}) copy-start(f32[512]{0:T(512)S(1)} %broadcast_multiply_fusion) | copy-start | bytes 6148
  481.6 34.8 %copy-start.57 = (f32[512]{0:T(512)}, f32[512]{0:T(512)S(1)}, u32[]{:S(2)}) copy-start(f32[512]{0:T(512)S(1)} %get-tuple-element.1195) | copy-start | bytes 6148
  481.6 34.8 %copy-start.67 = (f32[512]{0:T(512)}, f32[512]{0:T(512)S(1)}, u32[]{:S(2)}) copy-start(f32[512]{0:T(512)S(1)} %get-tuple-element.1194) | copy-start | bytes 6148
  665.0 299.5 %reduce-scatter.9.cloned.1.call-start = ((), (), s32[]{:S(2)}) async-start(), calls=%async_computation.12 | async-start | bytes 9437184 | tf_op jit(solution)/shard_map/reduce_scatter | solution.py:263
  801.1 187.2 %reduce-scatter.13.cloned.1.call-start = ((), (), s32[]{:S(2)}) async-start(), calls=%async_computation.14 | async-start | bytes 655360 | tf_op jit(solution)/shard_map/reduce_scatter | solution.py:286
  804.0 218.5 %reduce-scatter.15.cloned.1.call-start = ((), (), s32[]{:S(2)}) async-start(), calls=%async_computation.15 | async-start | bytes 2621440 | tf_op jit(solution)/shard_map/reduce_scatter | solution.py:289
  809.9 246.3 %reduce-scatter.17.cloned.1.call-start = ((), (), s32[]{:S(2)}) async-start(), calls=%async_computation.16 | async-start | bytes 2621440 | tf_op jit(solution)/shard_map/reduce_scatter | solution.py:292
  815.8 271.3 %reduce-scatter.11.cloned.1.call-start = ((), (), s32[]{:S(2)}) async-start(), calls=%async_computation.13 | async-start | bytes 1966080 | tf_op jit(solution)/shard_map/reduce_scatter | solution.py:283
  818.3 146.2 %copy-start.6 = (bf16[1,1,512,512]{2,3,1,0:T(8,128)(2,1)S(1)}, bf16[1,1,512,512]{2,3,1,0:T(8,128)(2,1)}, u32[]{:S(2)}) copy-start(bf16[1,1,512,512]{2,3,1,0:T(8,128)(2,1)} %copy-done.4) | copy-start | bytes 1572868
  818.3 146.2 %copy-start.64 = (f32[512]{0:T(512)S(1)}, f32[512]{0:T(512)}, u32[]{:S(2)}) copy-start(f32[512]{0:T(512)} %copy-done.63) | copy-start | bytes 6148
  818.3 146.2 %copy-start.70 = (f32[512]{0:T(512)S(1)}, f32[512]{0:T(512)}, u32[]{:S(2)}) copy-start(f32[512]{0:T(512)} %copy-done.69) | copy-start | bytes 6148
  826.8 260.4 %copy-start.101 = (u32[32]{0:T(128)S(1)}, u32[32]{0:T(128)}, u32[]{:S(2)}) copy-start(u32[32]{0:T(128)} %constant.231) | copy-start | bytes 388
  826.8 262.2 %copy-start.97 = (bf16[128]{0:T(256)(128)(2,1)S(1)}, bf16[128]{0:T(256)(128)(2,1)}, u32[]{:S(2)}) copy-start(bf16[128]{0:T(256)(128)(2,1)} %param.41) | copy-start | bytes 772
  969.1 202.5 %all-reduce.12.cloned.1.call-start = ((), (), s32[]{:S(2)}) async-start(), calls=%async_computation.18 | async-start | bytes 2359296 | tf_op jit(solution)/shard_map/psum | solution.py:319
  1056.3 178.0 %all-gather.27.cloned.1.call-start = ((), (), s32[]{:S(2)}) async-start(), calls=%async_computation.17 | async-start | bytes 3538944 | tf_op jit(solution)/shard_map/all_gather | solution.py:318
  1099.3 78.2 %copy-start.48 = (bf16[512,512]{1,0:T(8,128)(2,1)S(1)}, bf16[512,512]{1,0:T(8,128)(2,1)}, u32[]{:S(2)}) copy-start(bf16[512,512]{1,0:T(8,128)(2,1)} %copy.173) | copy-start | bytes 1572868
  (84 other events, 452.7 us)
Sparse Core Ops, SparseCore 0:
  9.6 22.3 all-gather.16
  36.9 125.5 all-gather.24
  164.7 123.1 all-gather.18
  289.3 20.7 all-gather.20
  311.5 22.5 all-gather.22
  665.2 147.1 reduce-scatter.6
  816.4 148.0 reduce-scatter.8
  967.6 20.6 reduce-scatter.12
  990.9 31.4 reduce-scatter.14
  1024.8 31.4 reduce-scatter.16
  1059.0 28.1 reduce-scatter.10
  1090.8 80.7 all-reduce.11
  1174.1 60.1 all-gather.26
